TPU v7x, 32 devices: a whole 2x2x4 slice. The times are simulated.
32 devices in a mesh: dp: 8 (over z, y), tp: 4 (over x, core).
Axes of the slice: x: 2, y: 2, z: 4, core: 2. Of those that a mesh axis runs over, the one named last changes fastest.
Arguments:
- tokens: bfloat16 [8, 2048, 768], P('dp', 'tp'), may hold values from -6 to 6
- cotangent: bfloat16 [8, 2048, 768], P('dp', 'tp'), may hold values from -6 to 6
- tags: int32 [8], P('dp'), may hold values from 0 to 7
- tag_weight: float32 [8], replicated, may hold values from 0.25 to 4
- query_weight: bfloat16 [768, 768], P(None, 'tp'), may hold values from -0.21875 to 0.21875
- key_value_weight: bfloat16 [768, 128], replicated, may hold values from -0.21875 to 0.21875
- output_weight: bfloat16 [768, 768], P('tp'), may hold values from -1.25 to 1.25
- up_weight: bfloat16 [768, 3072], P(None, 'tp'), may hold values from -0.21875 to 0.21875
- down_weight: bfloat16 [3072, 768], P('tp'), may hold values from -0.109375 to 0.109375
- norm_gain_one: float32 [768], replicated, may hold values from 0.25 to 1.75
- norm_bias_one: float32 [768], replicated, may hold values from -1.5 to 1.5
- norm_gain_two: float32 [768], replicated, may hold values from 0.25 to 1.75
- norm_bias_two: float32 [768], replicated, may hold values from -1.5 to 1.5
Outputs:
- block_out: bfloat16 [8, 2048, 768], P('dp', 'tp')
- grad_tokens: bfloat16 [8, 2048, 768], P('dp', 'tp')
- grad_query: float32 [768, 768], P(None, 'tp')
- grad_keyval: float32 [768, 128], replicated
- grad_output: float32 [768, 768], P('tp')
- grad_upward: float32 [768, 3072], P(None, 'tp')
- grad_downward: float32 [3072, 768], P('tp')
- grad_gain_one: float32 [768], replicated
- grad_bias_one: float32 [768], replicated
- grad_gain_two: float32 [768], replicated
- grad_bias_two: float32 [768], replicated
All inputs are finite; a program needn't handle non-finite values.
Results may differ from a plain program's by a relative error of at most 0.013.
Values may be sent and summed in bfloat16 or wider, within the bound.
A program may use at most 128 MiB of HBM per device.

v0:
```python
import jax
import jax.numpy as jnp
from jax import lax
from jax.sharding import PartitionSpec as P

HD = 64
ROT = 16


def layer_norm(values, gain_vec, shift_vec):
    row_mean = jnp.mean(values, axis=-1, keepdims=True)
    centred = values - row_mean
    variance = jnp.mean(centred * centred, axis=-1, keepdims=True)
    inverse = lax.rsqrt(variance + 1e-05)
    normal = centred * inverse
    return (normal * gain_vec + shift_vec, normal, inverse)


def norm_back(scaled, normal, inverse):
    term_one = jnp.mean(scaled, axis=-1, keepdims=True)
    term_two = jnp.mean(scaled * normal, axis=-1, keepdims=True)
    return inverse * (scaled - term_one - normal * term_two)


def rot_angles(positions):
    frequencies = 10000.0 ** (-jnp.arange(0, ROT, 2, dtype=jnp.float32) / ROT)
    return positions.astype(jnp.float32)[:, None] * frequencies[None, :]


def rotate(values, angles, direction):
    half_rot = ROT // 2
    cosine = jnp.cos(angles)[:, None, :]
    sine_part = direction * jnp.sin(angles)[:, None, :]
    front_half = values[..., :half_rot]
    back_half = values[..., half_rot:ROT]
    return jnp.concatenate(
        [
            front_half * cosine - back_half * sine_part,
            back_half * cosine + front_half * sine_part,
            values[..., ROT:],
        ],
        axis=-1,
    )


def outer_sum(left, right):
    return lax.dot_general(
        left, right, (((0, 1), (0, 1)), ((), ())), preferred_element_type=jnp.float32
    )


def against(left, weight):
    return lax.dot_general(
        left, weight, (((2,), (1,)), ((), ())), preferred_element_type=jnp.float32
    )


def shards(
    tokens,
    cotangent,
    tags,
    tag_weight,
    query_weight,
    key_value_weight,
    output_weight,
    up_weight,
    down_weight,
    norm_gain_one,
    norm_bias_one,
    norm_gain_two,
    norm_bias_two,
):
    seq_dev, own_len, model_width = tokens.shape
    full_len = own_len * lax.axis_size("tp")
    heads_dev = query_weight.shape[1] // HD
    score_scale = HD ** (-0.5)
    block_rows = min(512, full_len)
    blocks = full_len // block_rows
    own_rows = tokens.astype(jnp.float32)
    full_angles = rot_angles(jnp.arange(full_len))
    tag_ids = jnp.arange(tag_weight.shape[0], dtype=jnp.int32)
    row_weight = jnp.sum(
        jnp.where(tags[:, None] == tag_ids[None, :], tag_weight[None, :], 0.0), axis=1
    )
    upstream = cotangent.astype(jnp.float32) * row_weight[:, None, None]
    all_rows = lax.all_gather(tokens, "tp", axis=1, tiled=True).astype(jnp.float32)
    grad_rows = lax.all_gather(upstream.astype(jnp.bfloat16), "tp", axis=1, tiled=True)
    normed_one, normal_all, _ = layer_norm(all_rows, norm_gain_one, norm_bias_one)
    rows_one = normed_one.astype(jnp.bfloat16)
    rows_two = (normal_all * norm_gain_two + norm_bias_two).astype(jnp.bfloat16)
    key_value_rows = jnp.dot(rows_one, key_value_weight, preferred_element_type=jnp.float32)
    key_part = rotate(key_value_rows[:, :, None, :HD], full_angles, 1.0)[:, :, 0, :]
    key_value_rows = jnp.concatenate([key_part, key_value_rows[:, :, HD:]], axis=-1).astype(
        jnp.bfloat16
    )
    key_rows = key_value_rows[:, :, :HD]
    value_rows = key_value_rows[:, :, HD:]
    query_matrix = jnp.dot(rows_one, query_weight, preferred_element_type=jnp.float32).reshape(
        seq_dev, full_len, heads_dev, HD
    )
    query_matrix = rotate(query_matrix, full_angles, 1.0).astype(jnp.bfloat16)

    def block_scores(query_block, block_start):
        block_end = block_start + block_rows
        scores = (
            jnp.einsum(
                "sqhd,skd->sqhk",
                query_block,
                key_rows[:, :block_end],
                preferred_element_type=jnp.float32,
            )
            * score_scale
        )
        allowed = jnp.arange(block_end)[None, :] <= (block_start + jnp.arange(block_rows))[:, None]
        return jnp.where(allowed[None, :, None, :], scores, -1e30)

    context_list = []
    lse_list = []
    for block_index in range(blocks):
        block_start = block_index * block_rows
        block_end = block_start + block_rows
        scores = block_scores(query_matrix[:, block_start:block_end], block_start)
        row_top = jnp.max(scores, axis=-1, keepdims=True)
        weights = jnp.exp(scores - row_top)
        row_total = jnp.sum(weights, axis=-1, keepdims=True)
        weights_low = (weights / row_total).astype(jnp.bfloat16)
        context_list.append(
            jnp.einsum(
                "sqhk,skd->sqhd",
                weights_low,
                value_rows[:, :block_end],
                preferred_element_type=jnp.float32,
            )
        )
        lse_list.append(row_top + jnp.log(row_total))
    context_full = jnp.concatenate(context_list, axis=1)
    low_context = context_full.reshape(seq_dev, full_len, heads_dev * HD).astype(jnp.bfloat16)
    attention_branch = jnp.dot(low_context, output_weight, preferred_element_type=jnp.float32)
    hidden_rows = jnp.dot(rows_two, up_weight, preferred_element_type=jnp.float32)
    middle_rows = jax.nn.gelu(hidden_rows, approximate=False).astype(jnp.bfloat16)
    feedforward_branch = jnp.dot(middle_rows, down_weight, preferred_element_type=jnp.float32)
    branch = lax.psum_scatter(
        (attention_branch + feedforward_branch).astype(jnp.bfloat16),
        "tp",
        scatter_dimension=1,
        tiled=True,
    ).astype(jnp.float32)
    block_out = (own_rows + branch).astype(jnp.bfloat16)
    grad_output = outer_sum(low_context, grad_rows)
    grad_downward = outer_sum(middle_rows, grad_rows)
    grad_context = (
        against(grad_rows, output_weight)
        .astype(jnp.bfloat16)
        .reshape(seq_dev, full_len, heads_dev, HD)
    )
    grad_middle = against(grad_rows, down_weight)
    normal_cdf = 0.5 * (1.0 + lax.erf(hidden_rows * 0.7071067811865476))
    density = jnp.exp(-0.5 * hidden_rows * hidden_rows) * 0.3989422804014327
    grad_hidden = (grad_middle * (normal_cdf + hidden_rows * density)).astype(jnp.bfloat16)
    grad_upward = outer_sum(rows_two, grad_hidden)
    norm_part_two = against(grad_hidden, up_weight)
    grad_kv_full = jnp.zeros((seq_dev, full_len, 2 * HD), jnp.float32)
    query_grad_list = []
    for block_index in range(blocks):
        block_start = block_index * block_rows
        block_end = block_start + block_rows
        query_block = query_matrix[:, block_start:block_end]
        grad_block = grad_context[:, block_start:block_end]
        scores = block_scores(query_block, block_start)
        weights = jnp.exp(scores - lse_list[block_index])
        grad_weights = jnp.einsum(
            "sqhd,skd->sqhk",
            grad_block,
            value_rows[:, :block_end],
            preferred_element_type=jnp.float32,
        )
        row_delta = jnp.sum(
            grad_block.astype(jnp.float32) * context_list[block_index], axis=-1, keepdims=True
        )
        grad_scores = (weights * (grad_weights - row_delta)).astype(jnp.bfloat16)
        query_grad_list.append(
            jnp.einsum(
                "sqhk,skd->sqhd",
                grad_scores,
                key_rows[:, :block_end],
                preferred_element_type=jnp.float32,
            )
            * score_scale
        )
        grad_keys = (
            jnp.einsum(
                "sqhk,sqhd->skd", grad_scores, query_block, preferred_element_type=jnp.float32
            )
            * score_scale
        )
        grad_values = jnp.einsum(
            "sqhk,sqhd->skd",
            weights.astype(jnp.bfloat16),
            grad_block,
            preferred_element_type=jnp.float32,
        )
        grad_kv_full = grad_kv_full.at[:, :block_end].add(
            jnp.concatenate([grad_keys, grad_values], axis=-1)
        )
    grad_queries = jnp.concatenate(query_grad_list, axis=1)
    grad_queries = (
        rotate(grad_queries, full_angles, -1.0)
        .reshape(seq_dev, full_len, heads_dev * HD)
        .astype(jnp.bfloat16)
    )
    grad_query = outer_sum(rows_one, grad_queries)
    norm_part_one = against(grad_queries, query_weight)
    key_back = rotate(grad_kv_full[:, :, None, :HD], full_angles, -1.0)[:, :, 0, :]
    keyval_part = jnp.concatenate([key_back, grad_kv_full[:, :, HD:]], axis=-1)
    low_keyval = keyval_part.astype(jnp.bfloat16)
    grad_keyval = outer_sum(rows_one, low_keyval)
    part_one = norm_part_one + against(low_keyval, key_value_weight)
    small = jnp.stack(
        [
            jnp.sum(part_one * normal_all, axis=(0, 1)),
            jnp.sum(part_one, axis=(0, 1)),
            jnp.sum(norm_part_two * normal_all, axis=(0, 1)),
            jnp.sum(norm_part_two, axis=(0, 1)),
        ]
    )
    scaled = lax.psum_scatter(
        (part_one * norm_gain_one + norm_part_two * norm_gain_two).astype(jnp.bfloat16),
        "tp",
        scatter_dimension=1,
        tiled=True,
    ).astype(jnp.float32)
    _, normal_own, inverse_own = layer_norm(own_rows, norm_gain_one, norm_bias_one)
    grad_tokens = upstream + norm_back(scaled, normal_own, inverse_own)
    grad_query, grad_output, grad_upward, grad_downward = [
        v.astype(jnp.float32)
        for v in lax.psum(
            tuple(
                (
                    v.astype(jnp.bfloat16)
                    for v in (grad_query, grad_output, grad_upward, grad_downward)
                )
            ),
            "dp",
        )
    ]
    tail = lax.psum(
        jnp.concatenate([grad_keyval.reshape(-1), small.reshape(-1)]).reshape(-1, 128), ("dp", "tp")
    ).reshape(-1)
    grad_keyval, small = (
        tail[: grad_keyval.size].reshape(grad_keyval.shape),
        tail[grad_keyval.size :].reshape(small.shape),
    )
    grad_gain_one, grad_bias_one, grad_gain_two, grad_bias_two = small
    return (
        block_out,
        grad_tokens.astype(jnp.bfloat16),
        grad_query,
        grad_keyval,
        grad_output,
        grad_upward,
        grad_downward,
        grad_gain_one,
        grad_bias_one,
        grad_gain_two,
        grad_bias_two,
    )


def solution(mesh):
    in_specs = (
        P("dp", "tp", None),
        P("dp", "tp", None),
        P("dp"),
        P(),
        P(None, "tp"),
        P(),
        P("tp", None),
        P(None, "tp"),
        P("tp", None),
        P(),
        P(),
        P(),
        P(),
    )
    out_specs = (
        P("dp", "tp", None),
        P("dp", "tp", None),
        P(None, "tp"),
        P(),
        P("tp", None),
        P(None, "tp"),
        P("tp", None),
        P(),
        P(),
        P(),
        P(),
    )
    return jax.shard_map(shards, mesh=mesh, in_specs=in_specs, out_specs=out_specs, check_vma=False)
```

profile of v0, /device:TPU:0, one launch (start us, length us, event | category | flops | bytes accessed | tf_op | source)
XLA Modules:
  0.0 513.2 jit_solution(20159249226310110)
XLA Ops:
  8.6 1.3 fusion.171
  9.9 2.8 fusion.102
  12.8 0.8 iota_compare_fusion.5
  14.0 1.4 iota_compare_fusion.1
  16.0 1.0 broadcast_multiply_fusion
  17.0 23.9 %all-gather.3.cloned.1.call-done = bf16[1,2048,768]{2,1,0:T(8,128)(2,1)} async-done(((bf16[1,512,768]{2,1,0:T(8,128)(2,1)}), bf16[1,2048,768]{2,1,0:T(8,128)(2,1)}) %all-gather.3.cloned.1.call-update) | async-done | bytes 3145744 | tf_op jit(solution)/shard_map/all_gather | solution.py:86
  40.9 2.5 convert_reduce_fusion
  43.4 2.9 fusion.17
  47.0 1.5 fusion.12
  48.5 2.0 fusion.190
  50.9 1.2 fusion.68
  53.1 1.6 copy-done.7
  55.7 1.3 fusion.44
  57.1 1.8 fusion.38
  59.7 2.0 fusion.191
  61.7 6.2 %fusion.10 = (f32[512,3]{0,1:T(4,128)S(1)}, f32[512,3,2048]{2,0,1:T(8,128)}) fusion(pred[512,2048]{1,0:T(8,128)(4,1)S(1)} %iota_compare_fusion, bf16[1,2048,1,48]{1,3,2,0:T(8,128)(2,1)S(1)} %slice.387, bf16[1,2048,1,8]{1,3,2,0:T(8,128)(2,1)S(1)} %get-tuple-element.92, bf16[1,2048,1,8]{1,3,2,0:T(8,128)(2,1)S(1)} %get-tuple-element.91, ...), kind=kOutput, calls=%fused_computation.25 | convolution fusion | flops 412875264 | bytes 14096384 | tf_op jit(solution)/shard_map/sqhd,skd->sqhk/dot_general | solution.py:106
  67.9 1.2 copy-done.1
  69.0 1.4 fusion.2
  70.5 6.9 %fusion = f32[512,3]{0,1:T(4,128)S(1)} fusion(f32[512,3,2048]{2,0,1:T(8,128)} %get-tuple-element.109, f32[512,3]{0,1:T(4,128)S(1)} %get-tuple-element.108, pred[512,2048]{1,0:T(8,128)(4,1)S(1)} %iota_compare_fusion), kind=kLoop, calls=%fused_computation.6 | loop fusion | flops 12581376 | bytes 13643776 | tf_op jit(solution)/shard_map/reduce_sum | solution.py:125
  78.6 3.1 fusion.194
  82.2 2.9 fusion.193
  85.1 1.1 slice-done.8
  86.2 4.8 fusion.192
  91.0 3.1 fusion.71
  94.2 7.3 %fusion.80 = f32[1,2048,64]{1,2,0:T(8,128)} fusion(f32[512,3,2048]{2,0,1:T(8,128)} %get-tuple-element.109, f32[512,3]{0,1:T(4,128)S(1)} %copy-done.50, pred[512,2048]{1,0:T(8,128)(4,1)S(1)} %iota_compare_fusion, bf16[1,2048,3,64]{1,3,2,0:T(8,128)(2,1)S(1)} %bitcast.290), kind=kOutput, calls=%fused_computation.113 | convolution fusion | flops 415236096 | bytes 14360576 | tf_op jit(solution)/shard_map/sqhk,sqhd->skd/dot_general | solution.py:196
  101.6 2.0 fusion.132
  104.4 4.6 multiply_convert_fusion
  109.1 2.0 fusion.115
  111.1 1.2 fusion.84
  115.4 1.9 fusion.117
  117.3 2.4 multiply_convert_fusion.2
  120.4 1.1 fusion.113
  121.5 1.7 fusion.77
  123.2 2.5 multiply_convert_fusion.1
  125.7 0.9 fusion.86
  126.6 1.5 fusion.116
  129.3 0.8 copy-done.3
  130.1 17.6 %fusion.20 = (bf16[2048,768]{1,0:T(8,128)(2,1)}, f32[2048,768]{1,0:T(8,128)S(1)}) fusion(bf16[768,768]{1,0:T(8,128)(2,1)S(1)} %copy-done, bf16[1,2048,768]{2,1,0:T(8,128)(2,1)S(1)} %copy-done.3, f32[768]{0:T(1024)S(1)} %copy-done.59, f32[768]{0:T(1024)S(1)} %copy-done.55, f32[2048]{0:T(1024)S(1)} %copy-done.40, f32[2048]{0:T(1024)S(1)} %broadcast_multiply_fusion.1), kind=kOutput, calls=%fused_computation.35 | convolution fusion | flops 2527592448 | bytes 13785088 | tf_op jit(solution)/shard_map/dot_general | solution.py:139
  147.7 5.2 %fusion.26 = bf16[2048,768]{1,0:T(8,128)(2,1)S(1)} fusion(f32[2048,768]{1,0:T(8,128)S(1)} %get-tuple-element.112, bf16[768,768]{1,0:T(8,128)(2,1)S(1)} %copy-done.58, bf16[1,2048,768]{2,1,0:T(8,128)(2,1)S(1)} %copy-done.56), kind=kOutput, calls=%fused_computation.41 | convolution fusion | flops 2431647744 | bytes 13762560 | tf_op jit(solution)/shard_map/dot_general | solution.py:53
  152.9 2.7 fusion.197
  155.9 1.0 fusion.196
  156.9 0.8 copy-done.5
  157.7 1.0 convolution_bitcast_fusion
  158.8 3.0 fusion.15
  161.8 2.9 fusion.188
  164.7 0.8 maximum_bitcast_fusion
  165.8 7.1 %convolution_convert_fusion = bf16[768,768]{1,0:T(8,128)(2,1)} fusion(bf16[2048,768]{1,0:T(8,128)(2,1)} %copy-done.61, bf16[1,2048,768]{2,1,0:T(8,128)(2,1)} %all-gather.3.cloned.1.call-done, f32[768]{0:T(1024)S(1)} %copy-done.59, f32[768]{0:T(1024)S(1)} %copy-done.55, f32[2048]{0:T(1024)S(1)} %copy-done.40, f32[2048]{0:T(1024)S(1)} %broadcast_multiply_fusion.1), kind=kOutput, calls=%fused_computation.143 | convolution fusion | flops 2425946112 | bytes 7493632 | tf_op jit(solution)/shard_map/dot_general | solution.py:47
  173.0 3.7 fusion.104
  176.6 1.5 fusion.110
  178.2 1.5 fusion.107
  180.6 4.9 fusion.195
  185.5 2.7 fusion.65
  188.8 102.7 %all-reduce.5.cloned.1.call-done = f32[792,128]{1,0:T(8,128)} async-done(((f32[792,128]{1,0:T(8,128)}), f32[792,128]{1,0:T(8,128)}) %all-reduce.5.cloned.1.call-update) | async-done | bytes 405520 | tf_op jit(solution)/shard_map/psum | solution.py:246
  291.6 1.8 slice.289
  293.3 1.4 slice_bitcast_fusion.35
  294.7 127.7 %all-reduce.7.cloned.1.call-done = (bf16[768,192]{0,1:T(8,128)(2,1)}, bf16[192,768]{1,0:T(8,128)(2,1)}, bf16[768,768]{1,0:T(8,128)(2,1)}, bf16[768,768]{1,0:T(8,128)(2,1)}) async-done(((bf16[768,192]{0,1:T(8,128)(2,1)}, bf16[192,768]{1,0:T(8,128)(2,1)}, bf16[768,768]{1,0:T(8,128)(2,1)}, bf16[768,768]{1,0:T(8,128)(2,1)}), (bf16[768,192]{0,1:T(8,128)(2,1)}, bf16[192,768]{1,0:T(8,128)(2,1)}, ...) | async-done | bytes 2949136 | tf_op jit(solution)/shard_map/psum | solution.py:236
  422.5 1.8 convert_element_type.263
  424.3 1.8 convert_element_type.265
  426.1 2.8 convert_element_type.267
  428.9 2.9 convert_element_type.269
  431.8 29.9 %reduce-scatter.5.cloned.1.call-done = bf16[1,512,768]{2,1,0:T(8,128)(2,1)} async-done(((bf16[1,2048,768]{2,1,0:T(8,128)(2,1)}), bf16[1,512,768]{2,1,0:T(8,128)(2,1)}) %reduce-scatter.5.cloned.1.call-update) | async-done | bytes 786448 | tf_op jit(solution)/shard_map/reduce_scatter | solution.py:226
  461.7 1.9 convert_reduce_fusion.1
  463.6 38.7 %reduce-scatter.3.cloned.1.call-done = bf16[1,512,768]{2,1,0:T(8,128)(2,1)} async-done(((bf16[1,2048,768]{2,1,0:T(8,128)(2,1)}), bf16[1,512,768]{2,1,0:T(8,128)(2,1)}) %reduce-scatter.3.cloned.1.call-update) | async-done | bytes 786448 | tf_op jit(solution)/shard_map/reduce_scatter | solution.py:142
  502.2 3.8 fusion.93
  (221 shorter events, 15.0 us)
Async XLA Ops:
  7.2 122.1 %copy-start = (bf16[768,768]{1,0:T(8,128)(2,1)S(1)}, bf16[768,768]{1,0:T(8,128)(2,1)}, u32[]{:S(2)}) copy-start(bf16[768,768]{1,0:T(8,128)(2,1)} %param.30) | copy-start | bytes 3538948
  7.2 39.8 %copy-start.46 = (f32[768]{0:T(1024)S(1)}, f32[768]{0:T(1024)}, u32[]{:S(2)}) copy-start(f32[768]{0:T(1024)} %param.32) | copy-start | bytes 9220
  7.2 39.8 %copy-start.54 = (f32[768]{0:T(1024)S(1)}, f32[768]{0:T(1024)}, u32[]{:S(2)}) copy-start(f32[768]{0:T(1024)} %param.33) | copy-start | bytes 9220
  7.2 33.7 %all-gather.3.cloned.1.call-start = ((), (), s32[]{:S(2)}) async-start(), calls=%async_computation.2 | async-start | bytes 3932160 | tf_op jit(solution)/shard_map/all_gather | solution.py:86
  7.9 83.1 %all-gather.5.cloned.1.call-start = ((), (), s32[]{:S(2)}) async-start(), calls=%async_computation.4 | async-start | bytes 3932160 | tf_op jit(solution)/shard_map/all_gather | solution.py:87
  12.7 278.8 %all-reduce.5.cloned.1.call-start = ((), (), s32[]{:S(2)}) async-start(), calls=%async_computation.6 | async-start | bytes 811008 | tf_op jit(solution)/shard_map/psum | solution.py:246
  12.8 28.1 %copy-start.51 = (f32[8]{0:T(128)}, f32[8]{0:T(128)S(1)}, u32[]{:S(2)}) copy-start(f32[8]{0:T(128)S(1)} %multiply_power_fusion) | copy-start | bytes 100
  17.0 35.2 %copy-start.18 = (f32[2048,8]{0,1:T(8,128)}, f32[2048,8]{0,1:T(8,128)S(1)}, u32[]{:S(2)}) copy-start(f32[2048,8]{0,1:T(8,128)S(1)} %get-tuple-element.99) | copy-start | bytes 196612
  17.0 31.5 %copy-start.20 = (bf16[768,128]{1,0:T(8,128)(2,1)S(1)}, bf16[768,128]{1,0:T(8,128)(2,1)}, u32[]{:S(2)}) copy-start(bf16[768,128]{1,0:T(8,128)(2,1)} %param.28) | copy-start | bytes 589828
  40.9 6.1 %copy-start.2 = (bf16[1,2048,768]{2,1,0:T(8,128)(2,1)S(1)}, bf16[1,2048,768]{2,1,0:T(8,128)(2,1)}, u32[]{:S(2)}) copy-start(bf16[1,2048,768]{2,1,0:T(8,128)(2,1)} %all-gather.3.cloned.1.call-done) | copy-start | bytes 9437188
  46.4 4.2 copy-start.52
  47.0 3.9 copy-start.29
  48.5 3.6 copy-start.4
  50.9 10.8 %copy-start.25 = (bf16[1,2048,1,8]{1,3,2,0:T(8,128)(2,1)}, bf16[1,2048,1,8]{1,3,2,0:T(8,128)(2,1)S(1)}, u32[]{:S(2)}) copy-start(bf16[1,2048,1,8]{1,3,2,0:T(8,128)(2,1)S(1)} %get-tuple-element.91) | copy-start | bytes 98308
  50.9 10.8 %copy-start.27 = (bf16[1,2048,1,8]{1,3,2,0:T(8,128)(2,1)}, bf16[1,2048,1,8]{1,3,2,0:T(8,128)(2,1)S(1)}, u32[]{:S(2)}) copy-start(bf16[1,2048,1,8]{1,3,2,0:T(8,128)(2,1)S(1)} %get-tuple-element.92) | copy-start | bytes 98308
  50.9 10.8 %copy-start.12 = (bf16[1,2048,1,48]{1,3,2,0:T(8,128)(2,1)}, bf16[1,2048,1,48]{1,3,2,0:T(8,128)(2,1)S(1)}, u32[]{:S(2)}) copy-start(bf16[1,2048,1,48]{1,3,2,0:T(8,128)(2,1)S(1)} %slice.387) | copy-start | bytes 589828
  52.4 7.3 %copy-start.14 = (bf16[1,2048,64]{1,2,0:T(8,128)(2,1)}, bf16[1,2048,64]{1,2,0:T(8,128)(2,1)S(1)}, u32[]{:S(2)}) copy-start(bf16[1,2048,64]{1,2,0:T(8,128)(2,1)S(1)} %fusion.184) | copy-start | bytes 786436
  53.1 5.8 %copy-start.42 = (f32[512,3]{0,1:T(4,128)}, f32[512,3]{0,1:T(4,128)S(1)}, u32[]{:S(2)}) copy-start(f32[512,3]{0,1:T(4,128)S(1)} %get-tuple-element.100) | copy-start | bytes 18436
  55.1 3.8 copy-start.44
  55.7 3.9 copy-start.22
  57.1 21.4 %copy-start.10 = (f32[512,3,1024]{2,0,1:T(8,128)}, f32[512,3,1024]{2,0,1:T(8,128)S(1)}, u32[]{:S(2)}) copy-start(f32[512,3,1024]{2,0,1:T(8,128)S(1)} %get-tuple-element.105) | copy-start | bytes 18874372
  61.7 7.4 %copy-start.1 = (f32[512,3,1536]{2,0,1:T(8,128)}, f32[512,3,1536]{2,0,1:T(8,128)S(1)}, u32[]{:S(2)}) copy-start(f32[512,3,1536]{2,0,1:T(8,128)S(1)} %get-tuple-element.107) | copy-start | bytes 28311556
  70.4 8.1 %copy-start.16 = (bf16[1,2048,128]{1,2,0:T(8,128)(2,1)S(1)}, bf16[1,2048,128]{1,2,0:T(8,128)(2,1)}, u32[]{:S(2)}) copy-start(bf16[1,2048,128]{1,2,0:T(8,128)(2,1)} %get-tuple-element.102) | copy-start | bytes 1572868
  70.4 11.3 %slice-start = ((s8[9437184]{0:T(1024)(128)(4,1)}), s8[1048576]{0:T(1024)(128)(4,1)S(1)}, s32[]{:S(2)}) async-start(s8[9437184]{0:T(1024)(128)(4,1)} %bitcast.278), calls=%async_computation.8 | async-start | bytes 2097152
  78.5 3.2 slice-start.1
  78.5 3.7 slice-start.2
  78.5 6.6 %slice-start.6 = ((s8[12582912]{0:T(1024)(128)(4,1)}), s8[4194304]{0:T(1024)(128)(4,1)S(1)}, s32[]{:S(2)}) async-start(s8[12582912]{0:T(1024)(128)(4,1)} %bitcast.282), calls=%async_computation.14 | async-start | bytes 8388608
  78.6 6.6 %slice-start.7 = ((s8[12582912]{0:T(1024)(128)(4,1)}), s8[4194304]{0:T(1024)(128)(4,1)S(1)}, s32[]{:S(2)}) async-start(s8[12582912]{0:T(1024)(128)(4,1)} %bitcast.282), calls=%async_computation.15 | async-start | bytes 8388608
  82.2 4.0 slice-start.8
  91.0 3.1 copy-start.50
  94.1 7.4 %copy-start.8 = (f32[512,3,512]{0,2,1:T(8,128)S(1)}, f32[512,3,512]{0,2,1:T(8,128)}, u32[]{:S(2)}) copy-start(f32[512,3,512]{0,2,1:T(8,128)} %copy-done.7) | copy-start | bytes 9437188
  94.2 7.4 %copy-start.17 = (bf16[1,2048,128]{1,2,0:T(8,128)(2,1)S(1)}, bf16[1,2048,128]{1,2,0:T(8,128)(2,1)}, u32[]{:S(2)}) copy-start(bf16[1,2048,128]{1,2,0:T(8,128)(2,1)} %get-tuple-element.102) | copy-start | bytes 1572868
  94.2 7.4 %copy-start.43 = (f32[512,3]{0,1:T(4,128)S(1)}, f32[512,3]{0,1:T(4,128)}, u32[]{:S(2)}) copy-start(f32[512,3]{0,1:T(4,128)} %copy-done.42) | copy-start | bytes 18436
  94.2 7.4 %copy-start.45 = (f32[512,3]{0,1:T(4,128)S(1)}, f32[512,3]{0,1:T(4,128)}, u32[]{:S(2)}) copy-start(f32[512,3]{0,1:T(4,128)} %copy-done.44) | copy-start | bytes 18436
  94.2 7.4 %copy-start.62 = (f32[512,3,64]{0,2,1:T(8,128)S(1)}, f32[512,3,64]{0,2,1:T(8,128)}, u32[]{:S(2)}) copy-start(f32[512,3,64]{0,2,1:T(8,128)} %get-tuple-element.118) | copy-start | bytes 1179652
  94.2 7.4 %copy-start.63 = (f32[512,3,64]{0,2,1:T(8,128)S(1)}, f32[512,3,64]{0,2,1:T(8,128)}, u32[]{:S(2)}) copy-start(f32[512,3,64]{0,2,1:T(8,128)} %get-tuple-element.116) | copy-start | bytes 1179652
  94.2 7.4 %copy-start.64 = (f32[512,3,64]{0,2,1:T(8,128)S(1)}, f32[512,3,64]{0,2,1:T(8,128)}, u32[]{:S(2)}) copy-start(f32[512,3,64]{0,2,1:T(8,128)} %get-tuple-element.114) | copy-start | bytes 1179652
  94.2 9.4 %slice-start.9 = ((s8[12582912]{0:T(1024)(128)(4,1)}), s8[4194304]{0:T(1024)(128)(4,1)S(1)}, s32[]{:S(2)}) async-start(s8[12582912]{0:T(1024)(128)(4,1)} %bitcast.284), calls=%async_computation.17 | async-start | bytes 8388608
  94.2 9.4 %slice-start.10 = ((s8[12582912]{0:T(1024)(128)(4,1)}), s8[4194304]{0:T(1024)(128)(4,1)S(1)}, s32[]{:S(2)}) async-start(s8[12582912]{0:T(1024)(128)(4,1)} %bitcast.284), calls=%async_computation.18 | async-start | bytes 8388608
  104.4 4.6 copy-start.13
  104.4 4.6 copy-start.26
  104.4 4.7 copy-start.28
  109.0 3.3 copy-start.38
  117.3 4.2 slice-start.3
  117.3 4.2 slice-start.4
  120.4 2.8 copy-start.48
  130.1 17.6 %copy-start.56 = (bf16[1,2048,768]{2,1,0:T(8,128)(2,1)S(1)}, bf16[1,2048,768]{2,1,0:T(8,128)(2,1)}, u32[]{:S(2)}) copy-start(bf16[1,2048,768]{2,1,0:T(8,128)(2,1)} %all-gather.5.cloned.1.call-done) | copy-start | bytes 9437188
  130.1 17.6 %copy-start.58 = (bf16[768,768]{1,0:T(8,128)(2,1)S(1)}, bf16[768,768]{1,0:T(8,128)(2,1)}, u32[]{:S(2)}) copy-start(bf16[768,768]{1,0:T(8,128)(2,1)} %param.31) | copy-start | bytes 3538948
  152.9 2.8 copy-start.61
  152.9 3.0 copy-start.30
  155.9 2.9 copy-start.21
  158.8 3.0 copy-start.47
  165.5 257.0 %all-reduce.7.cloned.1.call-start = ((), (), s32[]{:S(2)}) async-start(), calls=%async_computation.7 | async-start | bytes 5898240 | tf_op jit(solution)/shard_map/psum | solution.py:236
  165.8 7.2 %copy-start.57 = (bf16[1,2048,768]{2,1,0:T(8,128)(2,1)S(1)}, bf16[1,2048,768]{2,1,0:T(8,128)(2,1)}, u32[]{:S(2)}) copy-start(bf16[1,2048,768]{2,1,0:T(8,128)(2,1)} %all-gather.5.cloned.1.call-done) | copy-start | bytes 9437188
  165.8 7.2 %copy-start.60 = (bf16[2048,768]{1,0:T(8,128)(2,1)S(1)}, bf16[2048,768]{1,0:T(8,128)(2,1)}, u32[]{:S(2)}) copy-start(bf16[2048,768]{1,0:T(8,128)(2,1)} %get-tuple-element.111) | copy-start | bytes 9437188
  172.9 3.7 copy-start.34
  172.9 3.7 copy-start.35
  172.9 3.7 copy-start.36
  172.9 3.7 copy-start.37
  172.9 5.2 %copy-start.6 = (bf16[1,2048,768]{2,1,0:T(8,128)(2,1)S(1)}, bf16[1,2048,768]{2,1,0:T(8,128)(2,1)}, u32[]{:S(2)}) copy-start(bf16[1,2048,768]{2,1,0:T(8,128)(2,1)} %copy-done.4) | copy-start | bytes 9437188
  179.7 282.0 %reduce-scatter.5.cloned.1.call-start = ((), (), s32[]{:S(2)}) async-start(), calls=%async_computation.5 | async-start | bytes 3932160 | tf_op jit(solution)/shard_map/reduce_scatter | solution.py:226
  180.3 5.2 %copy-start.31 = (bf16[192,768]{1,0:T(8,128)(2,1)S(1)}, bf16[192,768]{1,0:T(8,128)(2,1)}, u32[]{:S(2)}) copy-start(bf16[192,768]{1,0:T(8,128)(2,1)} %param.29) | copy-start | bytes 884740
  180.3 321.9 %reduce-scatter.3.cloned.1.call-start = ((), (), s32[]{:S(2)}) async-start(), calls=%async_computation.3 | async-start | bytes 3932160 | tf_op jit(solution)/shard_map/reduce_scatter | solution.py:142
  188.3 314.0 %copy-start.11 = (bf16[1,512,768]{2,1,0:T(8,128)(2,1)S(1)}, bf16[1,512,768]{2,1,0:T(8,128)(2,1)}, u32[]{:S(2)}) copy-start(bf16[1,512,768]{2,1,0:T(8,128)(2,1)} %param.24) | copy-start | bytes 2359300
  (21 other events, 41.6 us)
Sparse Core Ops, SparseCore 0:
  9.6 31.2 all-gather.2
  43.0 28.6 all-gather.4
  165.6 125.9 all-reduce.4
  296.6 125.8 all-reduce.6
  424.8 36.7 reduce-scatter.4
  464.2 37.9 reduce-scatter.2
where the time goes:
time: 517 us; the launch traced here: 513 us
  waiting for transfers between devices  324 us (63%)
  matrix products  111 us (21%)
  other arithmetic  49.1 us (9%)
  between operations  16.2 us (3%)
  local copies, waits for them, and re-layouts  11.6 us (2%)
    psum x1, waiting for transfers between devices, shards(): lax.psum(tuple((v.astype(jnp.bfloat16) for v in (grad_query, grad_output,...  128 us
    psum x1, waiting for transfers between devices, shards(): lax.psum(jnp.concatenate([grad_keyval.reshape(-1), small.reshape(-1)]).re...  103 us
    reduce_scatter x1, waiting for transfers between devices, shards(): lax.psum_scatter((attention_branch + feedforward_branch).astype(jnp.bfloa...  38.7 us
    reduce_scatter x1, waiting for transfers between devices, shards(): lax.psum_scatter((part_one * norm_gain_one + norm_part_two * norm_gain_tw...  29.9 us
    all_gather x1, waiting for transfers between devices, shards(): lax.all_gather(tokens, 'tp', axis=1, tiled=True).astype(jnp.float32)  23.9 us
    dot_general x1, matrix products, shards(): jnp.dot(rows_two, up_weight, preferred_element_type=jnp.float32)  17.6 us
    dot_general x5, matrix products, against(): lax.dot_general(left, weight, (((2,), (1,)), ((), ())), preferred_element...  15 us
    dot_general x5, matrix products, outer_sum(): lax.dot_general(left, right, (((0, 1), (0, 1)), ((), ())), preferred_elem...  14.9 us
  transfers between devices with their start and end apart: 6, of which 5 were waited for; matrix products, arithmetic and copies ran while one was open for 17% of the time, Pallas kernels for 0%

commit v1 on v0

--- a/solution.py
+++ b/solution.py
@@ -244,7 +244,10 @@
         )
     ]
     tail = lax.psum(
-        jnp.concatenate([grad_keyval.reshape(-1), small.reshape(-1)]).reshape(-1, 128), ("dp", "tp")
+        lax.psum(
+            jnp.concatenate([grad_keyval.reshape(-1), small.reshape(-1)]).reshape(-1, 128), "tp"
+        ),
+        "dp",
     ).reshape(-1)
     grad_keyval, small = (
         tail[: grad_keyval.size].reshape(grad_keyval.shape),

time: 517 us -> 497 us (0.961)
  waiting for transfers between devices: 324 us -> 301 us
    psum x1, waiting for transfers between devices: 103 us -> 21.5 us  [shards(): lax.psum(jnp.concatenate([grad_keyval.reshape(-1), small.reshape(-1)]).re...]
    psum x0 -> x1, waiting for transfers between devices: none -> 59.5 us  [shards(): lax.psum(lax.psum(jnp.concatenate([grad_keyval.reshape(-1), small.reshape...]
  transfers between devices with their start and end apart: 6 -> 7, of which waited for: 5 -> 6; matrix products, arithmetic and copies ran while one was open for 17% -> 19% of each run, Pallas kernels for 0% -> 0%
where the time goes in v1:
time: 497 us; the launch traced here: 494 us
  waiting for transfers between devices  301 us (61%)
  matrix products  115 us (23%)
  other arithmetic  49 us (10%)
  between operations  16.3 us (3%)
  local copies, waits for them, and re-layouts  11.7 us (2%)
    psum x1, waiting for transfers between devices, shards(): lax.psum(tuple((v.astype(jnp.bfloat16) for v in (grad_query, grad_output,...  126 us
    psum x1, waiting for transfers between devices, shards(): lax.psum(lax.psum(jnp.concatenate([grad_keyval.reshape(-1), small.reshape...  59.5 us
    reduce_scatter x1, waiting for transfers between devices, shards(): lax.psum_scatter((attention_branch + feedforward_branch).astype(jnp.bfloa...  38.6 us
    reduce_scatter x1, waiting for transfers between devices, shards(): lax.psum_scatter((part_one * norm_gain_one + norm_part_two * norm_gain_tw...  30 us
    all_gather x1, waiting for transfers between devices, shards(): lax.all_gather(tokens, 'tp', axis=1, tiled=True).astype(jnp.float32)  24 us
    psum x1, waiting for transfers between devices, shards(): lax.psum(jnp.concatenate([grad_keyval.reshape(-1), small.reshape(-1)]).re...  21.5 us
    dot_general x5, matrix products, outer_sum(): lax.dot_general(left, right, (((0, 1), (0, 1)), ((), ())), preferred_elem...  18.6 us
    dot_general x1, matrix products, shards(): jnp.dot(rows_two, up_weight, preferred_element_type=jnp.float32)  17.6 us
  transfers between devices with their start and end apart: 7, of which 6 were waited for; matrix products, arithmetic and copies ran while one was open for 19% of the time, Pallas kernels for 0%

profile of v1, /device:TPU:0, one launch (start us, length us, event | category | flops | bytes accessed | tf_op | source)
XLA Modules:
  0.0 493.5 jit_solution(11711842248145956900)
XLA Ops:
  8.6 1.3 fusion.171
  9.9 2.7 fusion.102
  12.8 0.8 iota_compare_fusion.5
  13.9 1.4 iota_compare_fusion.1
  15.9 1.0 broadcast_multiply_fusion
  16.9 24.0 %all-gather.3.cloned.1.call-done = bf16[1,2048,768]{2,1,0:T(8,128)(2,1)} async-done(((bf16[1,512,768]{2,1,0:T(8,128)(2,1)}), bf16[1,2048,768]{2,1,0:T(8,128)(2,1)}) %all-gather.3.cloned.1.call-update) | async-done | bytes 3145744 | tf_op jit(solution)/shard_map/all_gather | solution.py:86
  40.9 2.5 convert_reduce_fusion
  43.4 2.9 fusion.17
  47.0 1.5 fusion.12
  48.5 2.0 fusion.190
  50.9 1.2 fusion.68
  53.1 1.6 copy-done.6
  55.8 1.3 fusion.44
  57.1 1.8 fusion.38
  58.9 0.8 log_add_fusion.2
  59.8 2.0 fusion.191
  61.8 6.3 %fusion.10 = (f32[512,3]{0,1:T(4,128)S(1)}, f32[512,3,2048]{2,0,1:T(8,128)}) fusion(pred[512,2048]{1,0:T(8,128)(4,1)S(1)} %iota_compare_fusion, bf16[1,2048,1,48]{1,3,2,0:T(8,128)(2,1)S(1)} %slice.387, bf16[1,2048,1,8]{1,3,2,0:T(8,128)(2,1)S(1)} %get-tuple-element.92, bf16[1,2048,1,8]{1,3,2,0:T(8,128)(2,1)S(1)} %get-tuple-element.91, ...), kind=kOutput, calls=%fused_computation.25 | convolution fusion | flops 412875264 | bytes 14096384 | tf_op jit(solution)/shard_map/sqhd,skd->sqhk/dot_general | solution.py:106
  68.1 1.2 copy-done.1
  69.3 1.4 fusion.2
  70.7 6.9 %fusion = f32[512,3]{0,1:T(4,128)S(1)} fusion(f32[512,3,2048]{2,0,1:T(8,128)} %get-tuple-element.109, f32[512,3]{0,1:T(4,128)S(1)} %get-tuple-element.108, pred[512,2048]{1,0:T(8,128)(4,1)S(1)} %iota_compare_fusion), kind=kLoop, calls=%fused_computation.6 | loop fusion | flops 12581376 | bytes 13643776 | tf_op jit(solution)/shard_map/reduce_sum | solution.py:125
  78.8 3.1 fusion.194
  82.4 2.9 fusion.193
  85.3 1.1 slice-done.8
  86.4 4.8 fusion.192
  91.3 3.1 fusion.71
  94.5 7.3 %fusion.80 = f32[1,2048,64]{1,2,0:T(8,128)} fusion(f32[512,3,2048]{2,0,1:T(8,128)} %get-tuple-element.109, f32[512,3]{0,1:T(4,128)S(1)} %copy-done.49, pred[512,2048]{1,0:T(8,128)(4,1)S(1)} %iota_compare_fusion, bf16[1,2048,3,64]{1,3,2,0:T(8,128)(2,1)S(1)} %bitcast.290), kind=kOutput, calls=%fused_computation.113 | convolution fusion | flops 415236096 | bytes 14360576 | tf_op jit(solution)/shard_map/sqhk,sqhd->skd/dot_general | solution.py:196
  101.8 2.0 fusion.132
  104.6 4.6 multiply_convert_fusion
  109.3 2.0 fusion.115
  111.3 1.2 fusion.84
  115.6 1.9 fusion.117
  117.5 2.4 multiply_convert_fusion.2
  120.6 1.1 fusion.113
  121.7 1.7 fusion.77
  123.4 2.5 multiply_convert_fusion.1
  125.9 0.9 fusion.86
  126.8 1.5 fusion.116
  130.3 17.6 %fusion.20 = (bf16[2048,768]{1,0:T(8,128)(2,1)}, f32[2048,768]{1,0:T(8,128)S(1)}) fusion(bf16[768,768]{1,0:T(8,128)(2,1)S(1)} %copy-done, bf16[1,2048,768]{2,1,0:T(8,128)(2,1)S(1)} %copy-done.3, f32[768]{0:T(1024)S(1)} %copy-done.58, f32[768]{0:T(1024)S(1)} %copy-done.54, f32[2048]{0:T(1024)S(1)} %copy-done.39, f32[2048]{0:T(1024)S(1)} %broadcast_multiply_fusion.1), kind=kOutput, calls=%fused_computation.35 | convolution fusion | flops 2527592448 | bytes 13785088 | tf_op jit(solution)/shard_map/dot_general | solution.py:139
  147.9 5.2 %fusion.26 = bf16[2048,768]{1,0:T(8,128)(2,1)S(1)} fusion(f32[2048,768]{1,0:T(8,128)S(1)} %get-tuple-element.112, bf16[768,768]{1,0:T(8,128)(2,1)S(1)} %copy-done.57, bf16[1,2048,768]{2,1,0:T(8,128)(2,1)S(1)} %copy-done.55), kind=kOutput, calls=%fused_computation.41 | convolution fusion | flops 2431647744 | bytes 13762560 | tf_op jit(solution)/shard_map/dot_general | solution.py:53
  153.1 2.7 fusion.197
  156.1 1.0 fusion.196
  157.2 0.8 copy-done.5
  158.0 1.0 convolution_bitcast_fusion
  159.0 3.0 fusion.15
  162.0 2.8 fusion.188
  166.0 7.1 %convolution_convert_fusion = bf16[768,768]{1,0:T(8,128)(2,1)} fusion(bf16[2048,768]{1,0:T(8,128)(2,1)} %copy-done.60, bf16[1,2048,768]{2,1,0:T(8,128)(2,1)} %all-gather.3.cloned.1.call-done, f32[768]{0:T(1024)S(1)} %copy-done.58, f32[768]{0:T(1024)S(1)} %copy-done.54, f32[2048]{0:T(1024)S(1)} %copy-done.39, f32[2048]{0:T(1024)S(1)} %broadcast_multiply_fusion.1), kind=kOutput, calls=%fused_computation.143 | convolution fusion | flops 2425946112 | bytes 7493632 | tf_op jit(solution)/shard_map/dot_general | solution.py:47
  173.1 3.7 fusion.104
  176.8 21.5 %all-reduce.6.cloned.1.call-done = f32[792,128]{1,0:T(8,128)} async-done(((f32[792,128]{1,0:T(8,128)}), f32[792,128]{1,0:T(8,128)}) %all-reduce.6.cloned.1.call-update) | async-done | bytes 405520 | tf_op jit(solution)/shard_map/psum | solution.py:247
  198.4 3.4 fusion.107
  201.8 3.4 fusion.110
  206.1 4.9 fusion.195
  211.0 2.7 fusion.65
  214.3 59.5 %all-reduce.8.cloned.1.call-done = f32[792,128]{1,0:T(8,128)} async-done(((f32[792,128]{1,0:T(8,128)}), f32[792,128]{1,0:T(8,128)}) %all-reduce.8.cloned.1.call-update) | async-done | bytes 405520 | tf_op jit(solution)/shard_map/psum | solution.py:246
  273.9 1.8 slice.289
  275.7 1.4 slice_bitcast_fusion.35
  277.0 125.7 %all-reduce.10.cloned.1.call-done = (bf16[768,192]{0,1:T(8,128)(2,1)}, bf16[192,768]{1,0:T(8,128)(2,1)}, bf16[768,768]{1,0:T(8,128)(2,1)}, bf16[768,768]{1,0:T(8,128)(2,1)}) async-done(((bf16[768,192]{0,1:T(8,128)(2,1)}, bf16[192,768]{1,0:T(8,128)(2,1)}, bf16[768,768]{1,0:T(8,128)(2,1)}, bf16[768,768]{1,0:T(8,128)(2,1)}), (bf16[768,192]{0,1:T(8,128)(2,1)}, bf16[192,768]{1,0:T(8,128)(2,1)}, ...) | async-done | bytes 2949136 | tf_op jit(solution)/shard_map/psum | solution.py:236
  402.7 1.8 convert_element_type.263
  404.6 1.8 convert_element_type.265
  406.4 2.8 convert_element_type.267
  409.2 2.9 convert_element_type.269
  412.1 30.0 %reduce-scatter.5.cloned.1.call-done = bf16[1,512,768]{2,1,0:T(8,128)(2,1)} async-done(((bf16[1,2048,768]{2,1,0:T(8,128)(2,1)}), bf16[1,512,768]{2,1,0:T(8,128)(2,1)}) %reduce-scatter.5.cloned.1.call-update) | async-done | bytes 786448 | tf_op jit(solution)/shard_map/reduce_scatter | solution.py:226
  442.1 1.9 convert_reduce_fusion.1
  444.0 38.6 %reduce-scatter.3.cloned.1.call-done = bf16[1,512,768]{2,1,0:T(8,128)(2,1)} async-done(((bf16[1,2048,768]{2,1,0:T(8,128)(2,1)}), bf16[1,512,768]{2,1,0:T(8,128)(2,1)}) %reduce-scatter.3.cloned.1.call-update) | async-done | bytes 786448 | tf_op jit(solution)/shard_map/reduce_scatter | solution.py:142
  482.7 3.7 fusion.93
  (222 shorter events, 15.8 us)
Async XLA Ops:
  7.2 122.3 %copy-start = (bf16[768,768]{1,0:T(8,128)(2,1)S(1)}, bf16[768,768]{1,0:T(8,128)(2,1)}, u32[]{:S(2)}) copy-start(bf16[768,768]{1,0:T(8,128)(2,1)} %param.30) | copy-start | bytes 3538948
  7.2 39.8 %copy-start.45 = (f32[768]{0:T(1024)S(1)}, f32[768]{0:T(1024)}, u32[]{:S(2)}) copy-start(f32[768]{0:T(1024)} %param.32) | copy-start | bytes 9220
  7.2 39.8 %copy-start.53 = (f32[768]{0:T(1024)S(1)}, f32[768]{0:T(1024)}, u32[]{:S(2)}) copy-start(f32[768]{0:T(1024)} %param.33) | copy-start | bytes 9220
  7.2 33.7 %all-gather.3.cloned.1.call-start = ((), (), s32[]{:S(2)}) async-start(), calls=%async_computation.2 | async-start | bytes 3932160 | tf_op jit(solution)/shard_map/all_gather | solution.py:86
  7.9 83.3 %all-gather.5.cloned.1.call-start = ((), (), s32[]{:S(2)}) async-start(), calls=%async_computation.4 | async-start | bytes 3932160 | tf_op jit(solution)/shard_map/all_gather | solution.py:87
  12.6 185.6 %all-reduce.6.cloned.1.call-start = ((), (), s32[]{:S(2)}) async-start(), calls=%async_computation.6 | async-start | bytes 811008 | tf_op jit(solution)/shard_map/psum | solution.py:247
  12.7 28.2 %copy-start.50 = (f32[8]{0:T(128)}, f32[8]{0:T(128)S(1)}, u32[]{:S(2)}) copy-start(f32[8]{0:T(128)S(1)} %multiply_power_fusion) | copy-start | bytes 100
  16.9 35.3 %copy-start.17 = (f32[2048,8]{0,1:T(8,128)}, f32[2048,8]{0,1:T(8,128)S(1)}, u32[]{:S(2)}) copy-start(f32[2048,8]{0,1:T(8,128)S(1)} %get-tuple-element.99) | copy-start | bytes 196612
  16.9 31.6 %copy-start.19 = (bf16[768,128]{1,0:T(8,128)(2,1)S(1)}, bf16[768,128]{1,0:T(8,128)(2,1)}, u32[]{:S(2)}) copy-start(bf16[768,128]{1,0:T(8,128)(2,1)} %param.28) | copy-start | bytes 589828
  40.9 6.1 %copy-start.2 = (bf16[1,2048,768]{2,1,0:T(8,128)(2,1)S(1)}, bf16[1,2048,768]{2,1,0:T(8,128)(2,1)}, u32[]{:S(2)}) copy-start(bf16[1,2048,768]{2,1,0:T(8,128)(2,1)} %all-gather.3.cloned.1.call-done) | copy-start | bytes 9437188
  46.4 4.2 copy-start.51
  47.0 3.9 copy-start.28
  48.5 3.6 copy-start.4
  50.9 10.9 %copy-start.24 = (bf16[1,2048,1,8]{1,3,2,0:T(8,128)(2,1)}, bf16[1,2048,1,8]{1,3,2,0:T(8,128)(2,1)S(1)}, u32[]{:S(2)}) copy-start(bf16[1,2048,1,8]{1,3,2,0:T(8,128)(2,1)S(1)} %get-tuple-element.91) | copy-start | bytes 98308
  50.9 10.9 %copy-start.26 = (bf16[1,2048,1,8]{1,3,2,0:T(8,128)(2,1)}, bf16[1,2048,1,8]{1,3,2,0:T(8,128)(2,1)S(1)}, u32[]{:S(2)}) copy-start(bf16[1,2048,1,8]{1,3,2,0:T(8,128)(2,1)S(1)} %get-tuple-element.92) | copy-start | bytes 98308
  50.9 10.9 %copy-start.11 = (bf16[1,2048,1,48]{1,3,2,0:T(8,128)(2,1)}, bf16[1,2048,1,48]{1,3,2,0:T(8,128)(2,1)S(1)}, u32[]{:S(2)}) copy-start(bf16[1,2048,1,48]{1,3,2,0:T(8,128)(2,1)S(1)} %slice.387) | copy-start | bytes 589828
  52.4 7.4 %copy-start.13 = (bf16[1,2048,64]{1,2,0:T(8,128)(2,1)}, bf16[1,2048,64]{1,2,0:T(8,128)(2,1)S(1)}, u32[]{:S(2)}) copy-start(bf16[1,2048,64]{1,2,0:T(8,128)(2,1)S(1)} %fusion.184) | copy-start | bytes 786436
  53.1 5.8 %copy-start.41 = (f32[512,3]{0,1:T(4,128)}, f32[512,3]{0,1:T(4,128)S(1)}, u32[]{:S(2)}) copy-start(f32[512,3]{0,1:T(4,128)S(1)} %get-tuple-element.100) | copy-start | bytes 18436
  55.1 3.8 copy-start.43
  55.8 4.0 copy-start.21
  57.1 21.6 %copy-start.9 = (f32[512,3,1024]{2,0,1:T(8,128)}, f32[512,3,1024]{2,0,1:T(8,128)S(1)}, u32[]{:S(2)}) copy-start(f32[512,3,1024]{2,0,1:T(8,128)S(1)} %get-tuple-element.105) | copy-start | bytes 18874372
  61.8 7.5 %copy-start.1 = (f32[512,3,1536]{2,0,1:T(8,128)}, f32[512,3,1536]{2,0,1:T(8,128)S(1)}, u32[]{:S(2)}) copy-start(f32[512,3,1536]{2,0,1:T(8,128)S(1)} %get-tuple-element.107) | copy-start | bytes 28311556
  70.7 8.1 %copy-start.15 = (bf16[1,2048,128]{1,2,0:T(8,128)(2,1)S(1)}, bf16[1,2048,128]{1,2,0:T(8,128)(2,1)}, u32[]{:S(2)}) copy-start(bf16[1,2048,128]{1,2,0:T(8,128)(2,1)} %get-tuple-element.102) | copy-start | bytes 1572868
  70.7 11.2 %slice-start = ((s8[9437184]{0:T(1024)(128)(4,1)}), s8[1048576]{0:T(1024)(128)(4,1)S(1)}, s32[]{:S(2)}) async-start(s8[9437184]{0:T(1024)(128)(4,1)} %bitcast.278), calls=%async_computation.9 | async-start | bytes 2097152
  78.7 3.2 slice-start.1
  78.7 3.7 slice-start.2
  78.7 6.6 %slice-start.6 = ((s8[12582912]{0:T(1024)(128)(4,1)}), s8[4194304]{0:T(1024)(128)(4,1)S(1)}, s32[]{:S(2)}) async-start(s8[12582912]{0:T(1024)(128)(4,1)} %bitcast.282), calls=%async_computation.15 | async-start | bytes 8388608
  78.8 6.6 %slice-start.7 = ((s8[12582912]{0:T(1024)(128)(4,1)}), s8[4194304]{0:T(1024)(128)(4,1)S(1)}, s32[]{:S(2)}) async-start(s8[12582912]{0:T(1024)(128)(4,1)} %bitcast.282), calls=%async_computation.16 | async-start | bytes 8388608
  82.4 4.0 slice-start.8
  91.2 3.1 copy-start.49
  94.4 7.4 %copy-start.7 = (f32[512,3,512]{0,2,1:T(8,128)S(1)}, f32[512,3,512]{0,2,1:T(8,128)}, u32[]{:S(2)}) copy-start(f32[512,3,512]{0,2,1:T(8,128)} %copy-done.6) | copy-start | bytes 9437188
  94.4 7.4 %copy-start.16 = (bf16[1,2048,128]{1,2,0:T(8,128)(2,1)S(1)}, bf16[1,2048,128]{1,2,0:T(8,128)(2,1)}, u32[]{:S(2)}) copy-start(bf16[1,2048,128]{1,2,0:T(8,128)(2,1)} %get-tuple-element.102) | copy-start | bytes 1572868
  94.4 7.4 %copy-start.42 = (f32[512,3]{0,1:T(4,128)S(1)}, f32[512,3]{0,1:T(4,128)}, u32[]{:S(2)}) copy-start(f32[512,3]{0,1:T(4,128)} %copy-done.41) | copy-start | bytes 18436
  94.4 7.4 %copy-start.44 = (f32[512,3]{0,1:T(4,128)S(1)}, f32[512,3]{0,1:T(4,128)}, u32[]{:S(2)}) copy-start(f32[512,3]{0,1:T(4,128)} %copy-done.43) | copy-start | bytes 18436
  94.4 7.4 %copy-start.61 = (f32[512,3,64]{0,2,1:T(8,128)S(1)}, f32[512,3,64]{0,2,1:T(8,128)}, u32[]{:S(2)}) copy-start(f32[512,3,64]{0,2,1:T(8,128)} %get-tuple-element.118) | copy-start | bytes 1179652
  94.4 7.4 %copy-start.62 = (f32[512,3,64]{0,2,1:T(8,128)S(1)}, f32[512,3,64]{0,2,1:T(8,128)}, u32[]{:S(2)}) copy-start(f32[512,3,64]{0,2,1:T(8,128)} %get-tuple-element.116) | copy-start | bytes 1179652
  94.4 7.4 %copy-start.63 = (f32[512,3,64]{0,2,1:T(8,128)S(1)}, f32[512,3,64]{0,2,1:T(8,128)}, u32[]{:S(2)}) copy-start(f32[512,3,64]{0,2,1:T(8,128)} %get-tuple-element.114) | copy-start | bytes 1179652
  94.4 9.4 %slice-start.9 = ((s8[12582912]{0:T(1024)(128)(4,1)}), s8[4194304]{0:T(1024)(128)(4,1)S(1)}, s32[]{:S(2)}) async-start(s8[12582912]{0:T(1024)(128)(4,1)} %bitcast.284), calls=%async_computation.18 | async-start | bytes 8388608
  94.4 9.4 %slice-start.10 = ((s8[12582912]{0:T(1024)(128)(4,1)}), s8[4194304]{0:T(1024)(128)(4,1)S(1)}, s32[]{:S(2)}) async-start(s8[12582912]{0:T(1024)(128)(4,1)} %bitcast.284), calls=%async_computation.19 | async-start | bytes 8388608
  104.6 4.6 copy-start.12
  104.6 4.6 copy-start.25
  104.6 4.7 copy-start.27
  109.3 3.3 copy-start.37
  117.5 4.2 slice-start.3
  117.5 4.2 slice-start.4
  120.6 2.8 copy-start.47
  130.3 17.6 %copy-start.55 = (bf16[1,2048,768]{2,1,0:T(8,128)(2,1)S(1)}, bf16[1,2048,768]{2,1,0:T(8,128)(2,1)}, u32[]{:S(2)}) copy-start(bf16[1,2048,768]{2,1,0:T(8,128)(2,1)} %all-gather.5.cloned.1.call-done) | copy-start | bytes 9437188
  130.3 17.6 %copy-start.57 = (bf16[768,768]{1,0:T(8,128)(2,1)S(1)}, bf16[768,768]{1,0:T(8,128)(2,1)}, u32[]{:S(2)}) copy-start(bf16[768,768]{1,0:T(8,128)(2,1)} %param.31) | copy-start | bytes 3538948
  153.1 2.8 copy-start.60
  153.1 3.0 copy-start.29
  156.1 2.9 copy-start.20
  159.0 3.0 copy-start.46
  165.7 108.2 %all-reduce.8.cloned.1.call-start = ((), (), s32[]{:S(2)}) async-start(), calls=%async_computation.7 | async-start | bytes 811008 | tf_op jit(solution)/shard_map/psum | solution.py:246
  165.9 7.2 %copy-start.56 = (bf16[1,2048,768]{2,1,0:T(8,128)(2,1)S(1)}, bf16[1,2048,768]{2,1,0:T(8,128)(2,1)}, u32[]{:S(2)}) copy-start(bf16[1,2048,768]{2,1,0:T(8,128)(2,1)} %all-gather.5.cloned.1.call-done) | copy-start | bytes 9437188
  165.9 7.1 %copy-start.59 = (bf16[2048,768]{1,0:T(8,128)(2,1)S(1)}, bf16[2048,768]{1,0:T(8,128)(2,1)}, u32[]{:S(2)}) copy-start(bf16[2048,768]{1,0:T(8,128)(2,1)} %get-tuple-element.111) | copy-start | bytes 9437188
  173.1 28.6 %copy-start.33 = (bf16[512,3,64]{0,2,1:T(8,128)(2,1)S(1)}, bf16[512,3,64]{0,2,1:T(8,128)(2,1)}, u32[]{:S(2)}) copy-start(bf16[512,3,64]{0,2,1:T(8,128)(2,1)} %get-tuple-element.117) | copy-start | bytes 589828
  173.1 28.6 %copy-start.34 = (bf16[512,3,64]{0,2,1:T(8,128)(2,1)S(1)}, bf16[512,3,64]{0,2,1:T(8,128)(2,1)}, u32[]{:S(2)}) copy-start(bf16[512,3,64]{0,2,1:T(8,128)(2,1)} %get-tuple-element.115) | copy-start | bytes 589828
  173.1 28.6 %copy-start.35 = (bf16[512,3,64]{0,2,1:T(8,128)(2,1)S(1)}, bf16[512,3,64]{0,2,1:T(8,128)(2,1)}, u32[]{:S(2)}) copy-start(bf16[512,3,64]{0,2,1:T(8,128)(2,1)} %get-tuple-element.113) | copy-start | bytes 589828
  173.1 28.6 %copy-start.36 = (bf16[512,3,64]{0,2,1:T(8,128)(2,1)S(1)}, bf16[512,3,64]{0,2,1:T(8,128)(2,1)}, u32[]{:S(2)}) copy-start(bf16[512,3,64]{0,2,1:T(8,128)(2,1)} %get-tuple-element.110) | copy-start | bytes 589828
  198.3 204.4 %all-reduce.10.cloned.1.call-start = ((), (), s32[]{:S(2)}) async-start(), calls=%async_computation.8 | async-start | bytes 5898240 | tf_op jit(solution)/shard_map/psum | solution.py:236
  205.2 236.9 %reduce-scatter.5.cloned.1.call-start = ((), (), s32[]{:S(2)}) async-start(), calls=%async_computation.5 | async-start | bytes 3932160 | tf_op jit(solution)/shard_map/reduce_scatter | solution.py:226
  205.8 5.2 %copy-start.30 = (bf16[192,768]{1,0:T(8,128)(2,1)S(1)}, bf16[192,768]{1,0:T(8,128)(2,1)}, u32[]{:S(2)}) copy-start(bf16[192,768]{1,0:T(8,128)(2,1)} %param.29) | copy-start | bytes 884740
  205.8 276.9 %reduce-scatter.3.cloned.1.call-start = ((), (), s32[]{:S(2)}) async-start(), calls=%async_computation.3 | async-start | bytes 3932160 | tf_op jit(solution)/shard_map/reduce_scatter | solution.py:142
  213.8 268.9 %copy-start.10 = (bf16[1,512,768]{2,1,0:T(8,128)(2,1)S(1)}, bf16[1,512,768]{2,1,0:T(8,128)(2,1)}, u32[]{:S(2)}) copy-start(bf16[1,512,768]{2,1,0:T(8,128)(2,1)} %param.24) | copy-start | bytes 2359300
  (21 other events, 41.6 us)
Sparse Core Ops, SparseCore 0:
  9.6 31.2 all-gather.2
  43.0 28.5 all-gather.4
  165.8 32.4 all-reduce.5
  201.9 71.9 all-reduce.7
  278.4 124.3 all-reduce.9
  405.3 36.7 reduce-scatter.4
  444.7 37.9 reduce-scatter.2
